TPU v7x, 32 devices: a whole 2x2x4 slice. The times are simulated.
32 devices in a mesh: passage: 4 (over z), list: 8 (over y, x, core).
Axes of the slice: x: 2, y: 2, z: 4, core: 2. Of those that a mesh axis runs over, the one named last changes fastest.
Arguments:
- passages: bfloat16 [16384, 1024], P(('passage', 'list')), may hold values from -6 to 6
- list_ids: int32 [16384], P(('passage', 'list')), may hold values from 0 to 16383, as said below
- old_centroids: float32 [16384, 1024], P(('passage', 'list')), may hold values from -6 to 6
- rotation: float32 [1024, 1024], replicated, may hold values from -0.1875 to 0.1875
Outputs:
- rotated: bfloat16 [16384, 1024], P(('passage', 'list'))
- centroids: float32 [16384, 1024], P(('passage', 'list'))
Inputs may be any that keep to these rules, and one draw needn't show every extreme that they name: `list_ids`: on each device the ids of its 512 passages never fall. The lists o * 512 to (o + 1) * 512 - 1 belong to owner o, the device of index o along passage+list. At most 32 passages of one device fall in one owner's lists, and in every draw some owners take exactly 32 from every device.
All inputs are finite; a program needn't handle non-finite values.
Results may differ from a plain program's by a relative error of at most 0.001.
Values may be sent and summed in bfloat16 or wider, within the bound.
No kernel may reach another device: no remote copies, remote signals or barrier semaphores. Data moves between devices by JAX's collectives and lax.ppermute only.
A program may use at most 64 MiB of HBM per device.

v0:
```python
import jax
import jax.numpy as jnp
from jax import lax
from jax.sharding import PartitionSpec as P


def shards(passages, list_ids, old_centroids, rotation):
    n_pass = lax.axis_size("passage")
    n_list = lax.axis_size("list")
    devices = n_pass * n_list
    rows, width = passages.shape
    list_dev = old_centroids.shape[0]
    capacity = 2 * rows // devices
    owner_of = list_ids // list_dev
    owner_range = jnp.arange(devices, dtype=jnp.int32)
    loads = jnp.sum((owner_of[:, None] == owner_range[None, :]).astype(jnp.int32), axis=0)
    starts = jnp.cumsum(loads) - loads
    slot_range = jnp.arange(capacity, dtype=jnp.int32)
    source_row = starts[:, None] + slot_range[None, :]
    filled = slot_range[None, :] < loads[:, None]
    safe_row = jnp.clip(source_row, 0, rows - 1)
    outgoing = jnp.where(filled[:, :, None], passages[safe_row], jnp.zeros((), jnp.bfloat16))
    local_ids = jnp.where(filled, list_ids[safe_row] % list_dev, list_dev)
    got_rows, got_ids = (
        lax.all_to_all(outgoing, ("passage", "list"), split_axis=0, concat_axis=0, tiled=True),
        lax.all_to_all(local_ids, ("passage", "list"), split_axis=0, concat_axis=0, tiled=True),
    )
    flat_rows = got_rows.reshape(devices * capacity, width)
    flat_ids = got_ids.reshape(devices * capacity)
    list_range = jnp.arange(list_dev, dtype=jnp.int32)
    member = list_range[:, None] == flat_ids[None, :]
    sums = jnp.dot(member.astype(jnp.bfloat16), flat_rows, preferred_element_type=jnp.float32)
    tally = jnp.sum(member.astype(jnp.float32), axis=1)
    centroids = (sums + old_centroids) / (tally[:, None] + 1.0)
    safe_ids = jnp.clip(flat_ids, 0, list_dev - 1)
    back_index = owner_of * capacity + (jnp.arange(rows, dtype=jnp.int32) - starts[owner_of])
    residual = flat_rows.astype(jnp.float32) - jnp.take(centroids, safe_ids, axis=0)
    turned = jnp.dot(
        residual, rotation, preferred_element_type=jnp.float32, precision=lax.Precision.HIGHEST
    )
    turned = turned.astype(jnp.bfloat16).reshape(devices, capacity, width)
    returned = lax.all_to_all(turned, ("passage", "list"), split_axis=0, concat_axis=0, tiled=True)
    rotated = jnp.take(returned.reshape(devices * capacity, width), back_index, axis=0)
    return (rotated, centroids)


def solution(mesh):
    in_specs = (
        P(("passage", "list"), None),
        P(("passage", "list")),
        P(("passage", "list"), None),
        P(),
    )
    out_specs = (P(("passage", "list"), None), P(("passage", "list"), None))
    return jax.shard_map(shards, mesh=mesh, in_specs=in_specs, out_specs=out_specs, check_vma=False)
```

profile of v0, /device:TPU:0, one launch (start us, length us, event | category | flops | bytes accessed | tf_op | source)
XLA Modules:
  0.0 163.9 jit_solution(15360545222607063663)
XLA Ops:
  0.7 0.8 add_select_fusion
  1.4 0.1 convert_reduce_fusion.1
  2.0 6.9 %gather_fusion.1 = s32[1024]{0:T(1024)S(1)} fusion(s32[512]{0:T(512)S(1)} %copy-done.1, s32[1024]{0:T(1024)S(1)} %broadcast_clamp_fusion.1), kind=kCustom, calls=%fused_computation.1 | custom fusion | bytes 12288 | tf_op jit(solution)/shard_map/gather | solution.py:23
  8.9 0.7 compare_select_fusion.2
  9.7 7.3 %all-to-all-start.1 = ((s32[32,1,32]{2,1,0:T(1,128)}), s32[32,1,32]{2,1,0:T(1,128)S(1)}, u32[]{:S(2)}, u32[]{:S(2)}) async-start(s32[32,1,32]{2,1,0:T(1,128)} %compare_select_fusion.2), calls=%async_computation.1 | async-start | bytes 32768 | tf_op jit(solution)/shard_map/all_to_all | solution.py:26
  17.1 4.1 %gather_fusion = bf16[1024,1024]{1,0:T(8,128)(2,1)S(1)} fusion(bf16[512,1024]{1,0:T(8,128)(2,1)S(1)} %copy-done, s32[1024]{0:T(1024)S(1)} %broadcast_clamp_fusion.1), kind=kCustom, calls=%fused_computation | custom fusion | bytes 4198400 | tf_op jit(solution)/shard_map/gather | solution.py:22
  21.1 1.5 broadcast_select_fusion
  22.7 1.4 all-to-all-done.1
  24.1 4.4 %all-to-all-start = ((bf16[32,32,1024]{2,1,0:T(8,128)(2,1)}), bf16[32,32,1024]{2,1,0:T(8,128)(2,1)S(1)}, u32[]{:S(2)}, u32[]{:S(2)}) async-start(bf16[32,32,1024]{2,1,0:T(8,128)(2,1)} %broadcast_select_fusion), calls=%async_computation | async-start | bytes 4194304 | tf_op jit(solution)/shard_map/all_to_all | solution.py:25
  28.5 0.5 broadcast.359
  29.0 0.7 clamp_reduce_fusion
  29.9 0.3 convert_reduce_fusion
  30.3 47.0 %all-to-all-done = bf16[32,32,1024]{2,1,0:T(8,128)(2,1)S(1)} async-done(((bf16[32,32,1024]{2,1,0:T(8,128)(2,1)}), bf16[32,32,1024]{2,1,0:T(8,128)(2,1)S(1)}, u32[]{:S(2)}, u32[]{:S(2)}) %all-to-all-start) | async-done | bytes 2097184 | tf_op jit(solution)/shard_map/all_to_all | solution.py:25
  77.3 1.3 copy-done.3
  78.6 3.5 %add_divide_fusion = f32[512,1024]{1,0:T(8,128)S(1)} fusion(f32[512,1024]{1,0:T(8,128)} %param.6, bf16[1024,1024]{1,0:T(8,128)(2,1)} %bitcast.45, f32[512]{0:T(512)S(1)} %broadcast_add_fusion, s32[1024]{0:T(1024)S(1)} %reshape.212), kind=kOutput, calls=%fused_computation.10 | convolution fusion | flops 1075314688 | bytes 6297600 | tf_op jit(solution)/shard_map/dot_general | solution.py:32
  82.1 5.4 %gather_fusion.2 = f32[1024,1024]{1,0:T(8,128)} fusion(f32[512,1024]{1,0:T(8,128)S(1)} %add_divide_fusion, s32[1024]{0:T(1024)S(1)} %broadcast_clamp_fusion), kind=kCustom, calls=%fused_computation.2 | custom fusion | bytes 8392704 | tf_op jit(solution)/shard_map/jit(_take)/gather | solution.py:37
  87.5 18.4 %fusion.7 = bf16[1024,1024]{1,0:T(8,128)(2,1)} fusion(f32[1024,1024]{1,0:T(8,128)} %param.7, f32[1024,1024]{1,0:T(8,128)} %gather_fusion.2, bf16[1024,1024]{1,0:T(8,128)(2,1)} %bitcast.46, pred[1024]{0:T(1024)(128)(4,1)S(1)} %compare_and_fusion), kind=kOutput, calls=%fused_computation.15 | convolution fusion | flops 12889096192 | bytes 12583936 | tf_op jit(solution)/shard_map/dot_general | solution.py:38
  105.9 4.1 %all-to-all-start.2 = ((bf16[32,32,1024]{2,1,0:T(8,128)(2,1)}), bf16[32,32,1024]{2,1,0:T(8,128)(2,1)S(1)}, u32[]{:S(2)}, u32[]{:S(2)}) async-start(bf16[32,32,1024]{2,1,0:T(8,128)(2,1)} %bitcast.44), calls=%async_computation.2 | async-start | bytes 4194304 | tf_op jit(solution)/shard_map/all_to_all | solution.py:42
  110.0 0.7 fusion.18
  110.7 0.7 fusion.17
  111.5 20.1 %compare_and_fusion.1 = (pred[512]{0:T(512)(128)(4,1)S(1)}, s32[512]{0:T(512)S(1)}) fusion(s32[]{:T(128)} %bitcast.32, s32[]{:T(128)} %bitcast.31, s32[]{:T(128)} %bitcast.30, s32[]{:T(128)} %bitcast.29, s32[]{:T(128)} %bitcast.28, s32[]{:T(128)} %bitcast.27, s32[]{:T(128)} %bitcast.26, s32[]{:T(128)} %bitcast.25, s32[]{:T(128)} %bitcast.24, s32[]{:T(128)} %bitcast.23, ...), kind=kLoop, calls=%fused_computation.46 | loop fusion | flops 45568 | bytes 4736 | tf_op jit(solution)/shard_map/jit(_take)/and | solution.py:43
  131.6 27.2 %all-to-all-done.2 = bf16[32,32,1024]{2,1,0:T(8,128)(2,1)S(1)} async-done(((bf16[32,32,1024]{2,1,0:T(8,128)(2,1)}), bf16[32,32,1024]{2,1,0:T(8,128)(2,1)S(1)}, u32[]{:S(2)}, u32[]{:S(2)}) %all-to-all-start.2) | async-done | bytes 2097184 | tf_op jit(solution)/shard_map/all_to_all | solution.py:42
  158.8 2.8 %gather_fusion.3 = bf16[512,1024]{1,0:T(8,128)(2,1)} fusion(bf16[1024,1024]{1,0:T(8,128)(2,1)S(1)} %bitcast.42, s32[1024]{0:T(1024)S(1)} %pad_clamp_fusion), kind=kCustom, calls=%fused_computation.3 | custom fusion | bytes 2099200 | tf_op jit(solution)/shard_map/jit(_take)/gather | solution.py:43
  161.5 2.4 %broadcast_select_fusion.1 = bf16[512,1024]{1,0:T(8,128)(2,1)} fusion(bf16[512,1024]{1,0:T(8,128)(2,1)} %gather_fusion.3, pred[512]{0:T(512)(128)(4,1)S(1)} %get-tuple-element.4), kind=kLoop, calls=%fused_computation.17 | loop fusion | flops 524288 | bytes 2097664 | tf_op jit(solution)/shard_map/jit(_take)/select_n | solution.py:43
  (23 shorter events, 0.8 us)
Async XLA Ops:
  0.6 16.4 %copy-start = (bf16[512,1024]{1,0:T(8,128)(2,1)S(1)}, bf16[512,1024]{1,0:T(8,128)(2,1)}, u32[]{:S(2)}) copy-start(bf16[512,1024]{1,0:T(8,128)(2,1)} %param.4) | copy-start | bytes 3145732
  0.6 1.3 copy-start.1
  9.7 14.4 %all-to-all-start.1 = ((s32[32,1,32]{2,1,0:T(1,128)}), s32[32,1,32]{2,1,0:T(1,128)S(1)}, u32[]{:S(2)}, u32[]{:S(2)}) async-start(s32[32,1,32]{2,1,0:T(1,128)} %compare_select_fusion.2), calls=%async_computation.1 | async-start | bytes 32768 | tf_op jit(solution)/shard_map/all_to_all | solution.py:26
  24.1 53.2 %all-to-all-start = ((bf16[32,32,1024]{2,1,0:T(8,128)(2,1)}), bf16[32,32,1024]{2,1,0:T(8,128)(2,1)S(1)}, u32[]{:S(2)}, u32[]{:S(2)}) async-start(bf16[32,32,1024]{2,1,0:T(8,128)(2,1)} %broadcast_select_fusion), calls=%async_computation | async-start | bytes 4194304 | tf_op jit(solution)/shard_map/all_to_all | solution.py:25
  77.3 1.3 copy-start.3
  82.1 5.4 %copy-start.2 = (f32[512,1024]{1,0:T(8,128)}, f32[512,1024]{1,0:T(8,128)S(1)}, u32[]{:S(2)}) copy-start(f32[512,1024]{1,0:T(8,128)S(1)} %add_divide_fusion) | copy-start | bytes 6291460
  105.9 52.8 %all-to-all-start.2 = ((bf16[32,32,1024]{2,1,0:T(8,128)(2,1)}), bf16[32,32,1024]{2,1,0:T(8,128)(2,1)S(1)}, u32[]{:S(2)}, u32[]{:S(2)}) async-start(bf16[32,32,1024]{2,1,0:T(8,128)(2,1)} %bitcast.44), calls=%async_computation.2 | async-start | bytes 4194304 | tf_op jit(solution)/shard_map/all_to_all | solution.py:42
where the time goes:
time: 165 us; the launch traced here: 164 us
  waiting for transfers between devices  75.6 us (46%)
  other arithmetic  27 us (16%)
  local copies, waits for them, and re-layouts  22.8 us (14%)
  matrix products  21.9 us (13%)
  starting transfers between devices  15.8 us (10%)
    all_to_all x1, waiting for transfers between devices, shards(): lax.all_to_all(outgoing, ('passage', 'list'), split_axis=0, concat_axis=0...  47 us
    all_to_all x1, waiting for transfers between devices, shards(): lax.all_to_all(turned, ('passage', 'list'), split_axis=0, concat_axis=0,...  27.2 us
    and x1, other arithmetic, shards(): jnp.take(returned.reshape(devices * capacity, width), back_index, axis=0)  20.1 us
    dot_general x1, matrix products, shards(): jnp.dot(residual, rotation, preferred_element_type=jnp.float32, precision...  18.4 us
    all_to_all x1, starting transfers between devices, shards(): lax.all_to_all(local_ids, ('passage', 'list'), split_axis=0, concat_axis=...  7.33 us
    gather x2, local copies, waits for them, and re-layouts, shards(): local_ids = jnp.where(filled, list_ids[safe_row] % list_dev, list_dev)  6.95 us
    gather x1, local copies, waits for them, and re-layouts, shards(): jnp.take(centroids, safe_ids, axis=0)  5.43 us
    all_to_all x1, starting transfers between devices, shards(): lax.all_to_all(outgoing, ('passage', 'list'), split_axis=0, concat_axis=0...  4.42 us
  transfers between devices with their start and end apart: 3, of which 3 were waited for; matrix products, arithmetic and copies ran while one was open for 18% of the time, Pallas kernels for 0%

commit v1 on v0

v1 whole, which is shorter than its diff:
```python
import functools

import jax
import jax.numpy as jnp
from jax import lax
from jax.experimental import pallas as pl
from jax.experimental.pallas import tpu as pltpu
from jax.sharding import PartitionSpec as P

AXES = ("passage", "list")
BF16 = jnp.bfloat16
F32 = jnp.float32


def dot(a, b):
    return jnp.dot(a, b, preferred_element_type=F32)


def split3(value):
    high = value.astype(BF16)
    rest = value - high.astype(F32)
    middle = rest.astype(BF16)
    low = (rest - middle.astype(F32)).astype(BF16)
    return high, middle, low


def refine(chunk, rows_ref, ids_row_ref, ids_col_ref, old_ref, high_ref, low_ref, turned_ref, centroid_ref, parts_ref):
    slots = rows_ref.shape[0]
    lists = old_ref.shape[0]
    member = lax.broadcasted_iota(jnp.int32, (lists, slots), 0) == ids_row_ref[...]
    weight = member.astype(F32)
    tally = jnp.sum(weight, axis=1, keepdims=True)
    sums = dot(weight.astype(BF16), rows_ref[...])
    centroids = (sums + old_ref[...]) / (tally + 1.0)
    centroid_ref[...] = centroids
    for k, part in enumerate(split3(centroids)):
        parts_ref[k] = part

    def turn(step, carry):
        rows = pl.ds(pl.multiple_of(step * chunk, chunk), chunk)
        pick = lax.broadcasted_iota(jnp.int32, (chunk, lists), 1) == ids_col_ref[rows, :]
        pick = pick.astype(F32).astype(BF16)
        near = dot(pick, parts_ref[0]) + dot(pick, parts_ref[1]) + dot(pick, parts_ref[2])
        residual = rows_ref[rows, :].astype(F32) - near
        top = residual.astype(BF16)
        rest = (residual - top.astype(F32)).astype(BF16)
        out = dot(top, high_ref[...]) + (dot(top, low_ref[...]) + dot(rest, high_ref[...]))
        turned_ref[rows, :] = out.astype(BF16)
        return carry

    lax.fori_loop(0, slots // chunk, turn, 0)


def refined(rows, ids, old_centroids, high, low):
    slots, width = rows.shape
    lists = old_centroids.shape[0]
    chunk = 256 if slots % 256 == 0 else slots
    vmem = pl.BlockSpec(memory_space=pltpu.VMEM)
    return pl.pallas_call(
        functools.partial(refine, chunk),
        out_shape=(jax.ShapeDtypeStruct((slots, width), BF16), jax.ShapeDtypeStruct((lists, width), F32)),
        in_specs=[vmem] * 6,
        out_specs=(vmem, vmem),
        scratch_shapes=[pltpu.VMEM((3, lists, width), BF16)],
        compiler_params=pltpu.CompilerParams(vmem_limit_bytes=48 * 1024 * 1024),
        name="refine",
    )(rows, ids[None, :], ids[:, None], old_centroids, high, low)


def shards(passages, list_ids, old_centroids, rotation):
    devices = lax.axis_size("passage") * lax.axis_size("list")
    rows, width = passages.shape
    list_dev = old_centroids.shape[0]
    capacity = 2 * rows // devices
    owner_range = jnp.arange(devices, dtype=jnp.int32)
    starts = jnp.sum((list_ids[None, :] < (owner_range * list_dev)[:, None]).astype(jnp.int32), axis=1)
    slot_range = jnp.arange(capacity, dtype=jnp.int32)
    target = (starts[:, None] + slot_range[None, :]).reshape(-1)
    slot_owner = jnp.repeat(owner_range, capacity)
    select = (target[:, None] == jnp.arange(rows, dtype=jnp.int32)[None, :]) & (
        slot_owner[:, None] == (list_ids // list_dev)[None, :]
    )
    outgoing = dot(select.astype(BF16), passages).astype(BF16).reshape(devices, capacity, width)
    got_rows = lax.all_to_all(outgoing, AXES, split_axis=0, concat_axis=0, tiled=True)
    local = jnp.sum(jnp.where(select, (list_ids % list_dev - list_dev)[None, :], 0), axis=1) + list_dev
    got_ids = lax.all_to_all(local.reshape(devices, capacity), AXES, split_axis=0, concat_axis=0, tiled=True)
    high = lax.reduce_precision(rotation, 8, 7)
    low = (rotation - high).astype(BF16)
    high = high.astype(BF16)
    turned, centroids = refined(
        got_rows.reshape(devices * capacity, width), got_ids.reshape(-1), old_centroids, high, low
    )
    returned = lax.all_to_all(
        turned.reshape(devices, capacity, width), AXES, split_axis=0, concat_axis=0, tiled=True
    )
    rotated = lax.dot_general(
        select.astype(BF16),
        returned.reshape(devices * capacity, width),
        (((0,), (0,)), ((), ())),
        preferred_element_type=F32,
    ).astype(BF16)
    return rotated, centroids


def solution(mesh):
    in_specs = (P(AXES, None), P(AXES), P(AXES, None), P())
    out_specs = (P(AXES, None), P(AXES, None))
    return jax.shard_map(shards, mesh=mesh, in_specs=in_specs, out_specs=out_specs, check_vma=False)
```

time: 165 us -> 142 us (0.86)
  blocking collectives: 0 us -> 52.4 us
  waiting for transfers between devices: 75.6 us -> 45.5 us
  local copies, waits for them, and re-layouts: 22.8 us -> 3.82 us
  other arithmetic: 27 us -> 8.34 us
  matrix products: 21.9 us -> 5.13 us
  Pallas kernels: 0 us -> 15.3 us
  starting transfers between devices: 15.8 us -> 10.1 us
    all_to_all x0 -> x1, blocking collectives: none -> 52.4 us  [shards(): lax.all_to_all(turned.reshape(devices, capacity, width), AXES, split_axis...]
    all_to_all x3 -> x2, waiting for transfers between devices: 75.6 us -> 45.5 us  [the longest x1 41.1 us: shards(): lax.all_to_all(outgoing, AXES, split_axis=0, concat_axis=0, tiled=True)]
    gather x7 -> x0, local copies, waits for them, and re-layouts: 20.7 us -> none  [the longest x2 6.95 us: shards(): local_ids = jnp.where(filled, list_ids[safe_row] % list_dev, list_dev)]
    and x2 -> x0, other arithmetic: 20.1 us -> none  [the longest x1 20.1 us: shards(): jnp.take(returned.reshape(devices * capacity, width), back_index, axis=0)]
    dot_general x2, matrix products: 21.9 us -> 5.13 us  [the longest x1 2.72 us: dot(): return jnp.dot(a, b, preferred_element_type=F32)]
    pallas_call x0 -> x1, Pallas kernels: none -> 15.3 us  [refined(): pl.pallas_call(functools.partial(refine, chunk), out_shape=(jax.ShapeDtyp...]
    all_to_all x3 -> x2, starting transfers between devices: 15.8 us -> 10.1 us  [the longest x1 7.33 us: shards(): lax.all_to_all(local.reshape(devices, capacity), AXES, split_axis=0, conc...]
    select_n x6 -> x0, other arithmetic: 5.48 us -> none  [the longest x1 2.36 us: shards(): jnp.take(returned.reshape(devices * capacity, width), back_index, axis=0)]
  transfers between devices with their start and end apart: 3 -> 2, of which waited for: 3 -> 2; matrix products, arithmetic and copies ran while one was open for 18% -> 7% of each run, Pallas kernels for 0% -> 0%
where the time goes in v1:
time: 142 us; the launch traced here: 141 us
  blocking collectives  52.4 us (37%)
  waiting for transfers between devices  45.5 us (32%)
  Pallas kernels  15.3 us (11%)
  starting transfers between devices  10.1 us (7%)
  other arithmetic  8.34 us (6%)
  matrix products  5.13 us (4%)
  local copies, waits for them, and re-layouts  3.82 us (3%)
    all_to_all x1, blocking collectives, shards(): lax.all_to_all(turned.reshape(devices, capacity, width), AXES, split_axis...  52.4 us
    all_to_all x1, waiting for transfers between devices, shards(): lax.all_to_all(outgoing, AXES, split_axis=0, concat_axis=0, tiled=True)  41.1 us
    pallas_call x1, Pallas kernels, refined(): pl.pallas_call(functools.partial(refine, chunk), out_shape=(jax.ShapeDtyp...  15.3 us
    all_to_all x1, starting transfers between devices, shards(): lax.all_to_all(local.reshape(devices, capacity), AXES, split_axis=0, conc...  7.33 us
    convert_element_type x1, other arithmetic, shards(): low = (rotation - high).astype(BF16)  5.09 us
    all_to_all x1, waiting for transfers between devices, shards(): lax.all_to_all(local.reshape(devices, capacity), AXES, split_axis=0, conc...  4.38 us
  transfers between devices with their start and end apart: 2, of which 2 were waited for; matrix products, arithmetic and copies ran while one was open for 7% of the time, Pallas kernels for 0%

profile of v1, /device:TPU:0, one launch (start us, length us, event | category | flops | bytes accessed | tf_op | source)
XLA Modules:
  0.0 141.3 jit_solution(5433640018790949753)
XLA Ops:
  0.6 0.0 copy-start
  0.7 0.8 fusion.10
  1.4 0.9 convert_reduce_fusion
  2.3 0.1 iota_add_fusion
  2.4 0.1 add.48
  2.5 0.1 eq.33
  2.5 0.8 select_reduce_fusion
  3.4 0.7 add.52
  4.1 7.3 %all-to-all-start.1 = ((s32[32,1,32]{2,1,0:T(1,128)}), s32[32,1,32]{2,1,0:T(1,128)S(1)}, u32[]{:S(2)}, u32[]{:S(2)}) async-start(s32[32,1,32]{2,1,0:T(1,128)} %add.52), calls=%async_computation.1 | async-start | bytes 32768 | tf_op jit(solution)/shard_map/all_to_all | solution.py:86
  11.4 0.0 copy-done
  11.4 2.7 %convolution_convert_fusion = bf16[1024,1024]{1,0:T(8,128)(2,1)} fusion(bf16[512,1024]{1,0:T(8,128)(2,1)S(1)} %copy-done, s32[512]{0:T(512)S(1)} %get-tuple-element.9, s32[1024]{0:T(1024)S(1)} %add.48, s32[1024]{0:T(1024)S(1)} %eq.33), kind=kOutput, calls=%fused_computation.6 | convolution fusion | flops 1076363264 | bytes 3155968 | tf_op jit(solution)/shard_map/dot_general | solution.py:16
  14.1 4.4 %all-to-all-done.1 = s32[32,1,32]{2,1,0:T(1,128)S(1)} async-done(((s32[32,1,32]{2,1,0:T(1,128)}), s32[32,1,32]{2,1,0:T(1,128)S(1)}, u32[]{:S(2)}, u32[]{:S(2)}) %all-to-all-start.1) | async-done | bytes 4128 | tf_op jit(solution)/shard_map/all_to_all | solution.py:86
  18.5 2.7 %all-to-all-start = ((bf16[32,32,1024]{2,1,0:T(8,128)(2,1)}), bf16[32,32,1024]{2,1,0:T(8,128)(2,1)S(1)}, u32[]{:S(2)}, u32[]{:S(2)}) async-start(bf16[32,32,1024]{2,1,0:T(8,128)(2,1)} %bitcast.9), calls=%async_computation | async-start | bytes 4194304 | tf_op jit(solution)/shard_map/all_to_all | solution.py:84
  21.3 5.1 %fusion = (bf16[1024,1024]{1,0:T(8,128)(2,1)}, bf16[1024,1024]{1,0:T(8,128)(2,1)}) fusion(f32[1024,1024]{1,0:T(8,128)} %param.7), kind=kLoop, calls=%fused_computation.2 | loop fusion | flops 4194304 | bytes 8388608 | tf_op jit(solution)/shard_map/convert_element_type | solution.py:88
  26.3 0.5 broadcast.56
  26.9 0.7 reduce.5
  27.5 0.1 broadcast_in_dim_reshape.8.ids_row_ref
  27.6 1.3 broadcast_in_dim_reshape.10.ids_col_ref
  29.0 41.1 %all-to-all-done = bf16[32,32,1024]{2,1,0:T(8,128)(2,1)S(1)} async-done(((bf16[32,32,1024]{2,1,0:T(8,128)(2,1)}), bf16[32,32,1024]{2,1,0:T(8,128)(2,1)S(1)}, u32[]{:S(2)}, u32[]{:S(2)}) %all-to-all-start) | async-done | bytes 2097184 | tf_op jit(solution)/shard_map/all_to_all | solution.py:84
  70.1 0.0 copy-start.1
  70.1 1.0 copy-done.1
  71.1 15.3 %refine.1 = (bf16[1024,1024]{1,0:T(8,128)(2,1)S(1)}, f32[512,1024]{1,0:T(8,128)}) custom-call(bf16[1024,1024]{1,0:T(8,128)(2,1)S(1)} %bitcast.7, s32[1,1024]{1,0:T(1,128)S(1)} %broadcast_in_dim_reshape.8.ids_row_ref, s32[1024,1]{1,0:T(8,128)S(1)} %copy-done.1, f32[512,1024]{1,0:T(8,128)} %old_ref.1, bf16[1024,1024]{1,0:T(8,128)(2,1)} %get-tuple-element.7.high_ref, ...), custom_call_target="tpu_custom_call" | custom-call | tf_op jit(solution)/shard_map/refine/pallas_call | solution.py:59
  86.4 52.4 %all_to_all.16 = bf16[32,32,1024]{2,1,0:T(8,128)(2,1)S(1)} all-to-all(bf16[32,32,1024]{2,1,0:T(8,128)(2,1)S(1)} %bitcast.8), channel_id=1, replica_groups=mesh['passage'=4,'list'=8] {'passage','list'}, dimensions={0} | all-to-all | bytes 4194304 | tf_op jit(solution)/shard_map/all_to_all | solution.py:93
  138.9 2.4 %convolution_convert_fusion.1 = bf16[512,1024]{1,0:T(8,128)(2,1)} fusion(bf16[1024,1024]{1,0:T(8,128)(2,1)S(1)} %bitcast.10, s32[512]{0:T(512)S(1)} %get-tuple-element.9, s32[1024]{0:T(1024)S(1)} %add.48, s32[1024]{0:T(1024)S(1)} %eq.33), kind=kOutput, calls=%fused_computation.7 | convolution fusion | flops 1075838976 | bytes 3155968 | tf_op jit(solution)/shard_map/dot_general | solution.py:96
  (3 shorter events, 0.0 us)
Async XLA Ops:
  0.6 10.8 %copy-start = (bf16[512,1024]{1,0:T(8,128)(2,1)S(1)}, bf16[512,1024]{1,0:T(8,128)(2,1)}, u32[]{:S(2)}) copy-start(bf16[512,1024]{1,0:T(8,128)(2,1)} %param.4) | copy-start | bytes 3145732
  4.1 14.4 %all-to-all-start.1 = ((s32[32,1,32]{2,1,0:T(1,128)}), s32[32,1,32]{2,1,0:T(1,128)S(1)}, u32[]{:S(2)}, u32[]{:S(2)}) async-start(s32[32,1,32]{2,1,0:T(1,128)} %add.52), calls=%async_computation.1 | async-start | bytes 32768 | tf_op jit(solution)/shard_map/all_to_all | solution.py:86
  18.5 51.6 %all-to-all-start = ((bf16[32,32,1024]{2,1,0:T(8,128)(2,1)}), bf16[32,32,1024]{2,1,0:T(8,128)(2,1)S(1)}, u32[]{:S(2)}, u32[]{:S(2)}) async-start(bf16[32,32,1024]{2,1,0:T(8,128)(2,1)} %bitcast.9), calls=%async_computation | async-start | bytes 4194304 | tf_op jit(solution)/shard_map/all_to_all | solution.py:84
  70.1 1.0 copy-start.1

commit v2 on v1

v2 whole, which is shorter than its diff:
```python
import functools

import jax
import jax.numpy as jnp
from jax import lax
from jax.experimental import pallas as pl
from jax.experimental.pallas import tpu as pltpu
from jax.sharding import PartitionSpec as P


AXES = ("passage", "list")
BF16 = jnp.bfloat16
F32 = jnp.float32
I32 = jnp.int32
VMEM = pl.BlockSpec(memory_space=pltpu.VMEM)
SMEM = pl.BlockSpec(memory_space=pltpu.SMEM)
TILE = 16


def dot(a, b):
    return jnp.dot(a, b, preferred_element_type=F32)


def iota(shape, axis):
    return lax.broadcasted_iota(I32, shape, axis)


def hot(condition):
    return condition.astype(F32).astype(BF16)


def split3(value):
    high = value.astype(BF16)
    rest = value - high.astype(F32)
    middle = rest.astype(BF16)
    low = (rest - middle.astype(F32)).astype(BF16)
    return high, middle, low


LIMIT = 24
CENTRE = 48


def centred(rows, ids, parts_ref):
    pick = hot(iota((rows.shape[0], parts_ref.shape[1]), 1) == ids)
    near = dot(pick, parts_ref[0]) + dot(pick, parts_ref[1]) + dot(pick, parts_ref[2])
    residual = rows.astype(F32) - near
    top = residual.astype(BF16)
    return top, (residual - top.astype(F32)).astype(BF16)


def turned(top, rest, high_ref, low_ref):
    out = dot(top, high_ref[...]) + (dot(top, low_ref[...]) + dot(rest, high_ref[...]))
    return out.astype(BF16)


def means(row_ref, old_ref, centroid_ref, parts_ref, pieces):
    lists = old_ref.shape[0]
    ids = row_ref[...]
    weight = (iota((lists, ids.shape[1]), 0) == ids).astype(F32)
    tally = jnp.sum(weight, axis=1, keepdims=True)
    weight = weight.astype(BF16)
    sums = None
    for begin, rows in pieces:
        part = dot(weight[:, begin : begin + rows.shape[0]], rows)
        sums = part if sums is None else sums + part
    centroids = (sums + old_ref[...]) / (tally + 1.0)
    centroid_ref[...] = centroids
    for k, part in enumerate(split3(centroids)):
        parts_ref[k] = part


def refine(chunk, rows_ref, row_ref, col_ref, old_ref, high_ref, low_ref, turned_ref, centroid_ref, parts_ref):
    means(row_ref, old_ref, centroid_ref, parts_ref, [(0, rows_ref[...])])

    def body(step, carry):
        rows = pl.ds(pl.multiple_of(step * chunk, chunk), chunk)
        top, rest = centred(rows_ref[rows, :], col_ref[rows, :], parts_ref)
        turned_ref[rows, :] = turned(top, rest, high_ref, low_ref)
        return carry

    lax.fori_loop(0, rows_ref.shape[0] // chunk, body, 0)


def ranks(devices, lists, ids):
    owner = ids // lists
    order = iota((devices, ids.shape[1]), 0)
    mine = order == owner
    starts = jnp.sum((ids < order * lists).astype(F32), axis=1, keepdims=True)
    start = jnp.sum(jnp.where(mine, starts, 0.0), axis=0, keepdims=True).astype(I32)
    return owner, iota(ids.shape, 1) - start, mine


def pack_ids(devices, capacity, lists, ids_ref, local_ref):
    ids = ids_ref[...]
    _, rank, mine = ranks(devices, lists, ids)
    rank = hot(iota((capacity, ids.shape[1]), 0) == rank)
    code = ids % lists + 1
    step = 32
    total = None
    for piece, scale in ((code // step, step), (code % step, 1)):
        part = jnp.where(mine, piece.astype(F32), 0.0).astype(BF16)
        found = lax.dot_general(part, rank, (((1,), (1,)), ((), ())), preferred_element_type=F32) * scale
        total = found if total is None else total + found
    local_ref[...] = total.astype(I32) - 1


def pack_far(devices, capacity, lists, group, me_ref, ids_ref, passages_ref, slot_ref, *out_refs):
    half = devices // 2
    owner, rank, _ = ranks(devices, lists, ids_ref[...])
    relative = jnp.bitwise_xor(owner, me_ref[0])
    block = jnp.where(relative >= half, relative - half, half + jnp.bitwise_and(owner, half - 1))
    slot = block * capacity + rank
    slot_ref[...] = slot
    size = out_refs[0].shape[0]
    for g in range(len(out_refs) // group):
        begin, count = g * group * size, group * size
        select = hot(iota((count, slot.shape[1]), 0) + begin == slot)
        rows = dot(select, passages_ref[...]).astype(BF16)
        for k in range(group):
            out_refs[g * group + k][...] = rows[k * size : (k + 1) * size]


def pack_near(slot_ref, passages_ref, out_ref):
    size = out_ref.shape[0]
    select = hot(iota((size, slot_ref.shape[1]), 0) + size == slot_ref[...])
    out_ref[...] = dot(select, passages_ref[...]).astype(BF16)


def gather_far(capacity, direct_refs, swap_refs, rows_ref):
    for k, (direct, swap) in enumerate(zip(direct_refs, swap_refs)):
        at = 2 * k * capacity
        rows_ref[at : at + capacity] = direct[0:capacity]
        rows_ref[at + capacity : at + 2 * capacity] = swap[capacity : 2 * capacity]


def spread(rows, out_refs):
    size = out_refs[0].shape[0]
    for k, ref in enumerate(out_refs):
        ref[...] = rows[k * size : (k + 1) * size]


def centre(pairs, first, capacity, *refs):
    direct_refs, swap_refs, refs = refs[:pairs], refs[pairs : 2 * pairs], refs[2 * pairs :]
    near_ref, row_ref, col_ref, old_ref, high_ref, low_ref, centroid_ref, parts_ref, held_ref = refs[:9]
    out_refs = refs[9:]
    gather_far(capacity, direct_refs, swap_refs, held_ref)
    far = held_ref.shape[0]
    means(row_ref, old_ref, centroid_ref, parts_ref, [(0, held_ref[...]), (far, near_ref[...])])
    count = 2 * first * capacity
    top, rest = centred(held_ref[0:count], col_ref[0:count], parts_ref)
    spread(turned(top, rest, high_ref, low_ref), out_refs)


def turn_far(begin, held_ref, col_ref, parts_ref, high_ref, low_ref, *out_refs):
    count = sum(ref.shape[0] for ref in out_refs)
    top, rest = centred(held_ref[begin : begin + count], col_ref[begin : begin + count], parts_ref)
    spread(turned(top, rest, high_ref, low_ref), out_refs)


def turn_near(chunks, near_ref, col_ref, parts_ref, high_ref, low_ref, out_ref):
    begin = col_ref.shape[0] - near_ref.shape[0]
    size = near_ref.shape[0] // chunks
    for c in range(chunks):
        at = c * size
        top, rest = centred(near_ref[at : at + size], col_ref[begin + at : begin + at + size], parts_ref)
        out_ref[at : at + size] = turned(top, rest, high_ref, low_ref)


def unpack(pairs, capacity, *refs):
    direct_refs, swap_refs, refs = refs[:pairs], refs[pairs : 2 * pairs], refs[2 * pairs :]
    near_ref, slot_ref, out_ref, rows_ref = refs
    gather_far(capacity, direct_refs, swap_refs, rows_ref)
    far, size = rows_ref.shape[0], slot_ref.shape[0]
    pick = hot(iota((size, far), 1) == slot_ref[...])
    other = hot(iota((size, near_ref.shape[0]), 1) + far == slot_ref[...])
    out_ref[...] = (dot(pick, rows_ref[...]) + dot(other, near_ref[...])).astype(BF16)


def call(body, inputs, outputs, scratch=(), flops=0, limit=LIMIT):
    outs = [jax.ShapeDtypeStruct(shape, kind) for shape, kind in outputs]
    size = sum(a.size * a.dtype.itemsize for a in list(inputs) + outs)
    return pl.pallas_call(
        body,
        out_shape=outs,
        in_specs=[SMEM if a.shape == (1,) else VMEM for a in inputs],
        out_specs=[VMEM] * len(outs),
        scratch_shapes=[pltpu.VMEM(shape, kind) for shape, kind in scratch],
        compiler_params=pltpu.CompilerParams(vmem_limit_bytes=limit * 1024 * 1024),
        cost_estimate=pl.CostEstimate(flops=flops, bytes_accessed=size, transcendentals=0),
    )(*inputs)


def split_rotation(rotation):
    high = lax.reduce_precision(rotation, 8, 7)
    low = (rotation - high).astype(BF16)
    return high.astype(BF16), low


def whole_exchange(passages, list_ids, old_centroids, rotation, devices, capacity):
    rows, width = passages.shape
    lists = old_centroids.shape[0]
    slots = devices * capacity
    owners = jnp.arange(devices, dtype=I32)
    starts = jnp.sum((list_ids[None, :] < (owners * lists)[:, None]).astype(I32), axis=1)
    target = (starts[:, None] + jnp.arange(capacity, dtype=I32)[None, :]).reshape(-1)
    select = (target[:, None] == jnp.arange(rows, dtype=I32)[None, :]) & (
        jnp.repeat(owners, capacity)[:, None] == (list_ids // lists)[None, :]
    )
    outgoing = dot(select.astype(BF16), passages).astype(BF16).reshape(devices, capacity, width)
    got_rows = lax.all_to_all(outgoing, AXES, 0, 0, tiled=True)
    local = jnp.sum(jnp.where(select, (list_ids % lists - lists)[None, :], 0), axis=1) + lists
    ids = lax.all_to_all(local.reshape(devices, capacity), AXES, 0, 0, tiled=True).reshape(-1)
    high, low = split_rotation(rotation)
    chunk = 256 if slots % 256 == 0 else slots
    result, centroids = call(
        functools.partial(refine, chunk),
        (got_rows.reshape(slots, width), ids[None, :], ids[:, None], old_centroids, high, low),
        [((slots, width), BF16), ((lists, width), F32)],
        scratch=[((3, lists, width), BF16)],
        limit=48,
    )
    returned = lax.all_to_all(result.reshape(devices, capacity, width), AXES, 0, 0, tiled=True)
    rotated = lax.dot_general(
        select.astype(BF16), returned.reshape(slots, width), (((0,), (0,)), ((), ())), preferred_element_type=F32
    )
    return rotated.astype(BF16), centroids


def shards(passages, list_ids, old_centroids, rotation):
    devices = lax.axis_size("passage") * lax.axis_size("list")
    rows, width = passages.shape
    lists = old_centroids.shape[0]
    capacity = 2 * rows // devices
    if not by_halves(devices, capacity):
        return whole_exchange(passages, list_ids, old_centroids, rotation, devices, capacity)
    half = devices // 2
    pairs = half // 2
    far = half * capacity
    pair = ((2 * capacity, width), BF16)
    unit = 2 * width * width
    me = lax.axis_index(AXES).astype(I32)
    base = jnp.bitwise_and(me, half)
    ids = list_ids[None, :]
    groups = [list(range(half)), list(range(half, devices))]
    rings = [[(i, i ^ (half + 2 * k)) for i in range(devices)] for k in range(pairs)]
    chip = [(i, i ^ 1) for i in range(devices)]

    def shift(a, ring):
        return lax.ppermute(a, AXES, ring)

    def swap_near(a):
        return lax.all_to_all(
            a.reshape(half, capacity, -1), AXES, 0, 0, tiled=True, axis_index_groups=groups
        ).reshape(a.shape)

    def swap_cores(arrived):
        return [shift(a, chip) for a in arrived]

    packed = call(
        functools.partial(pack_far, devices, capacity, lists, pairs // 2),
        (me[None], ids, passages),
        [((1, rows), I32)] + [pair] * pairs,
        limit=62,
        flops=unit * far * rows // width,
    )
    slot = packed[0]
    direct = [shift(a, rings[k]) for k, a in enumerate(packed[1:])]
    local = call(functools.partial(pack_ids, devices, capacity, lists), (ids,), [((devices, capacity), I32)])[0]
    near = call(pack_near, (slot, passages), [((far, width), BF16)], flops=unit * far * rows // width)[0]
    near_rows = swap_near(near)
    got = lax.all_to_all(local, AXES, 0, 0, tiled=True)
    far_ids = jnp.take(got, jnp.bitwise_xor(jnp.arange(half, dtype=I32) + half, me), axis=0, mode="clip")
    near_ids = lax.dynamic_slice_in_dim(got, base, half, 0)
    ids_of_slots = jnp.concatenate([far_ids, near_ids]).reshape(-1)
    col_ids = ids_of_slots[:, None]
    row_ids = ids_of_slots[None, :]
    high, low = split_rotation(rotation)
    slot_col = slot.reshape(rows, 1)
    swapped = swap_cores(direct)

    first = 2
    parts_kind = ((3, lists, width), BF16)
    results = call(
        functools.partial(centre, pairs, first, capacity),
        (*direct, *swapped, near_rows, row_ids, col_ids, old_centroids, high, low),
        [((lists, width), F32), parts_kind, ((far, width), BF16)] + [pair] * first,
        limit=CENTRE,
        flops=unit * 600,
    )
    centroids, parts, held = results[:3]
    back = [shift(a, rings[k]) for k, a in enumerate(results[3:])]
    more = call(
        functools.partial(turn_far, 2 * first * capacity),
        (held, col_ids, parts, high, low),
        [pair] * (pairs - first),
        flops=unit * 1000,
    )
    back += [shift(a, rings[first + k]) for k, a in enumerate(more)]
    result = call(
        functools.partial(turn_near, 2),
        (near_rows, col_ids, parts, high, low),
        [((far, width), BF16)],
        flops=unit * 1500,
    )[0]
    near_back = swap_near(result)
    swapped = swap_cores(back)
    rotated = call(
        functools.partial(unpack, pairs, capacity),
        (*back, *swapped, near_back, slot_col),
        [((rows, width), BF16)],
        scratch=[((far, width), BF16)],
        flops=unit * 512,
    )[0]
    return rotated, centroids


def by_halves(devices, capacity):
    return capacity % TILE == 0 and devices % 16 == 0 and devices & (devices - 1) == 0


def solution(mesh):
    in_specs = (P(AXES, None), P(AXES), P(AXES, None), P())
    out_specs = (P(AXES, None), P(AXES, None))
    return jax.shard_map(shards, mesh=mesh, in_specs=in_specs, out_specs=out_specs, check_vma=False)
```

time: 142 us -> 174 us (1.23)
  starting transfers between devices: 10.1 us -> 64.9 us
  blocking collectives: 52.4 us -> 0 us
  local copies, waits for them, and re-layouts: 3.82 us -> 24.4 us
  Pallas kernels: 15.3 us -> 24.9 us
  waiting for transfers between devices: 45.5 us -> 52.5 us
  matrix products: 5.13 us -> 0 us
  other arithmetic: 8.34 us -> 5.71 us
    all_to_all x1 -> x0, blocking collectives: 52.4 us -> none  [shards(): lax.all_to_all(turned.reshape(devices, capacity, width), AXES, split_axis...]
    ppermute x0 -> x32, waiting for transfers between devices: none -> 50.4 us  [shift(): return lax.ppermute(a, AXES, ring)]
    ppermute x0 -> x32, starting transfers between devices: none -> 49.4 us  [shift(): return lax.ppermute(a, AXES, ring)]
    all_to_all x2 -> x3, waiting for transfers between devices: 45.5 us -> 2.04 us  [the longest x1 2.04 us: shards(): got = lax.all_to_all(local, AXES, 0, 0, tiled=True)]
    unnamed x4 -> x82, local copies, waits for them, and re-layouts: 1.05 us -> 21.6 us
    pallas_call x1 -> x7, Pallas kernels: 15.3 us -> 24.9 us  [call(): pl.pallas_call(body, out_shape=outs, in_specs=[SMEM if a.shape == (1,) el...]
    all_to_all x2 -> x3, starting transfers between devices: 10.1 us -> 15.5 us  [the longest x2 8.17 us: swap_near(): lax.all_to_all(a.reshape(half, capacity, -1), AXES, 0, 0, tiled=True, axi...]
    dot_general x2 -> x0, matrix products: 5.13 us -> none  [the longest x1 2.72 us: dot(): return jnp.dot(a, b, preferred_element_type=F32)]
  transfers between devices with their start and end apart: 2 -> 35, of which waited for: 2 -> 13; matrix products, arithmetic and copies ran while one was open for 7% -> 5% of each run, Pallas kernels for 0% -> 5%
where the time goes in v2:
time: 174 us; the launch traced here: 173 us
  starting transfers between devices  64.9 us (37%)
  waiting for transfers between devices  52.5 us (30%)
  Pallas kernels  24.9 us (14%)
  local copies, waits for them, and re-layouts  24.4 us (14%)
  other arithmetic  5.71 us (3%)
    ppermute x32, waiting for transfers between devices, shift(): return lax.ppermute(a, AXES, ring)  50.4 us
    ppermute x32, starting transfers between devices, shift(): return lax.ppermute(a, AXES, ring)  49.4 us
    pallas_call x7, Pallas kernels, call(): pl.pallas_call(body, out_shape=outs, in_specs=[SMEM if a.shape == (1,) el...  24.9 us
    unnamed x82, local copies, waits for them, and re-layouts  21.6 us
    all_to_all x2, starting transfers between devices, swap_near(): lax.all_to_all(a.reshape(half, capacity, -1), AXES, 0, 0, tiled=True, axi...  8.17 us
    all_to_all x1, starting transfers between devices, shards(): got = lax.all_to_all(local, AXES, 0, 0, tiled=True)  7.32 us
    convert_element_type x1, other arithmetic, split_rotation(): low = (rotation - high).astype(BF16)  5.1 us
  transfers between devices with their start and end apart: 35, of which 13 were waited for; matrix products, arithmetic and copies ran while one was open for 5% of the time, Pallas kernels for 5%

profile of v2, /device:TPU:0, one launch (start us, length us, event | category | flops | bytes accessed | tf_op | source)
XLA Modules:
  0.0 173.3 jit_solution(17270986090718628414)
XLA Ops:
  2.3 7.3 %all-to-all-start.1 = ((s32[32,1,32]{2,1,0:T(1,128)}), s32[32,1,32]{2,1,0:T(1,128)S(1)}, u32[]{:S(2)}, u32[]{:S(2)}) async-start(s32[32,1,32]{2,1,0:T(1,128)} %bitcast.5), calls=%async_computation.1 | async-start | bytes 32768 | tf_op jit(solution)/shard_map/all_to_all | solution.py:272
  9.6 2.8 %shard_map.59 = (s32[1,512]{1,0:T(1,128)}, bf16[64,1024]{1,0:T(8,128)(2,1)}, bf16[64,1024]{1,0:T(8,128)(2,1)}, bf16[64,1024]{1,0:T(8,128)(2,1)}, bf16[64,1024]{1...) custom-call(s32[1]{0:T(128)} %bitcast.me_ref, ...), custom_call_target="tpu_custom_call" | custom-call | flops 536870912 | bytes 2101252 | tf_op jit(solution)/shard_map/pallas_call | solution.py:183
  16.8 3.7 %all-to-all-start = ((bf16[16,32,1024]{2,1,0:T(8,128)(2,1)}), bf16[16,32,1024]{2,1,0:T(8,128)(2,1)S(1)}, u32[]{:S(2)}, u32[]{:S(2)}) async-start(bf16[16,32,1024]{2,1,0:T(8,128)(2,1)} %bitcast.2), calls=%async_computation | async-start | bytes 2097152 | tf_op jit(solution)/shard_map/all_to_all | solution.py:253
  20.4 3.1 %collective-permute-start.2 = (bf16[64,1024]{1,0:T(8,128)(2,1)S(1)}, bf16[64,1024]{1,0:T(8,128)(2,1)S(1)}, u32[]{:S(2)}, u32[]{:S(2)}) collective-permute-start(bf16[64,1024]{1,0:T(8,128)(2,1)S(1)} %copy-done.40), channel_id=1, source_target_pairs={{0,20},{1,21},{2,22},{3,23},{4,16},{5,17},{6,18},{7,19},{8,28},{9,... | collective-permute-start | bytes 393224 | tf_op jit(solution)/shard_map/ppermute | solution.py:250
  25.6 2.7 %collective-permute-start.4 = (bf16[64,1024]{1,0:T(8,128)(2,1)S(1)}, bf16[64,1024]{1,0:T(8,128)(2,1)S(1)}, u32[]{:S(2)}, u32[]{:S(2)}) collective-permute-start(bf16[64,1024]{1,0:T(8,128)(2,1)S(1)} %copy-done.38), channel_id=1, source_target_pairs={{0,24},{1,25},{2,26},{3,27},{4,28},{5,29},{6,30},{7,31},{8,16},{9,... | collective-permute-start | bytes 393224 | tf_op jit(solution)/shard_map/ppermute | solution.py:250
  29.1 4.0 %collective-permute-start.6 = (bf16[64,1024]{1,0:T(8,128)(2,1)S(1)}, bf16[64,1024]{1,0:T(8,128)(2,1)S(1)}, u32[]{:S(2)}, u32[]{:S(2)}) collective-permute-start(bf16[64,1024]{1,0:T(8,128)(2,1)S(1)} %copy-done.36), channel_id=1, source_target_pairs={{0,28},{1,29},{2,30},{3,31},{4,24},{5,25},{6,26},{7,27},{8,20},{9,... | collective-permute-start | bytes 393224 | tf_op jit(solution)/shard_map/ppermute | solution.py:250
  33.1 3.9 %collective-permute-done.2.refs_2_ = bf16[64,1024]{1,0:T(8,128)(2,1)S(1)} collective-permute-done((bf16[64,1024]{1,0:T(8,128)(2,1)S(1)}, bf16[64,1024]{1,0:T(8,128)(2,1)S(1)}, u32[]{:S(2)}, u32[]{:S(2)}) %collective-permute-start.2) | collective-permute-done | bytes 131104 | tf_op jit(solution)/shard_map/ppermute | solution.py:250
  37.0 3.7 %collective-permute-start.7 = (bf16[64,1024]{1,0:T(8,128)(2,1)}, bf16[64,1024]{1,0:T(8,128)(2,1)S(1)}, u32[]{:S(2)}, u32[]{:S(2)}) collective-permute-start(bf16[64,1024]{1,0:T(8,128)(2,1)} %get-tuple-element.29), channel_id=1, source_target_pairs={{0,30},{1,31},{2,28},{3,29},{4,26},{5,27},{6,24},{7,25},{8,22},{9,... | collective-permute-start | bytes 393224 | tf_op jit(solution)/shard_map/ppermute | solution.py:250
  40.7 5.1 %fusion = (bf16[1024,1024]{1,0:T(8,128)(2,1)}, bf16[1024,1024]{1,0:T(8,128)(2,1)}) fusion(f32[1024,1024]{1,0:T(8,128)} %param.7), kind=kLoop, calls=%fused_computation.3 | loop fusion | flops 4194304 | bytes 8388608 | tf_op jit(solution)/shard_map/convert_element_type | solution.py:196
  48.8 2.8 %collective-permute-done.6.refs_6_ = bf16[64,1024]{1,0:T(8,128)(2,1)S(1)} collective-permute-done((bf16[64,1024]{1,0:T(8,128)(2,1)S(1)}, bf16[64,1024]{1,0:T(8,128)(2,1)S(1)}, u32[]{:S(2)}, u32[]{:S(2)}) %collective-permute-start.6) | collective-permute-done | bytes 131104 | tf_op jit(solution)/shard_map/ppermute | solution.py:250
  51.6 3.6 %collective-permute-done.7.refs_7_ = bf16[64,1024]{1,0:T(8,128)(2,1)S(1)} collective-permute-done((bf16[64,1024]{1,0:T(8,128)(2,1)}, bf16[64,1024]{1,0:T(8,128)(2,1)S(1)}, u32[]{:S(2)}, u32[]{:S(2)}) %collective-permute-start.7) | collective-permute-done | bytes 131104 | tf_op jit(solution)/shard_map/ppermute | solution.py:250
  55.3 13.2 %collective-permute-done.refs_0_ = bf16[64,1024]{1,0:T(8,128)(2,1)S(1)} collective-permute-done((bf16[64,1024]{1,0:T(8,128)(2,1)S(1)}, bf16[64,1024]{1,0:T(8,128)(2,1)S(1)}, u32[]{:S(2)}, u32[]{:S(2)}) %collective-permute-start) | collective-permute-done | bytes 131104 | tf_op jit(solution)/shard_map/ppermute | solution.py:250
  68.5 3.5 %collective-permute-done.1.refs_1_ = bf16[64,1024]{1,0:T(8,128)(2,1)S(1)} collective-permute-done((bf16[64,1024]{1,0:T(8,128)(2,1)S(1)}, bf16[64,1024]{1,0:T(8,128)(2,1)S(1)}, u32[]{:S(2)}, u32[]{:S(2)}) %collective-permute-start.1) | collective-permute-done | bytes 131104 | tf_op jit(solution)/shard_map/ppermute | solution.py:250
  88.3 7.0 %shard_map.62 = (f32[512,1024]{1,0:T(8,128)}, bf16[3,512,1024]{2,1,0:T(8,128)(2,1)}, bf16[512,1024]{1,0:T(8,128)(2,1)S(1)}, bf16[64,1024]{1,0:T(8,128)(2,1)S(1)}, bf16[64,1024]{1,0:T(8,128)(2,1)S(1)}) custom-call(bf16[64,1024]{1,0:T(8,128)(2,1)S(1)} %collective-permute-done.refs_0_, bf16[64,1024]{1,0:T(8,128)(2,1)S(1)} %copy-done.12, ...), custom_call_target="tpu_custom_call" | custom-call | flops 1258291200 | bytes 15998976 | tf_op jit(solution)/shard_map/pallas_call | solution.py:183
  97.7 5.2 %shard_map.64 = bf16[512,1024]{1,0:T(8,128)(2,1)S(1)} custom-call(bf16[512,1024]{1,0:T(8,128)(2,1)S(1)} %bitcast.15, s32[1024,1]{1,0:T(8,128)S(1)} %broadcast_in_dim_reshape.8.refs_18_.col_ref, bf16[3,512,1024]{2,1,0:T(8,128)(2,1)S(1)} %copy-done.5, bf16[1024,1024]{1,0:T(8,128)(2,1)S(1)} %copy-done.1, bf16[1024,1024]{1,0:T(8,128)(2,1)S(1)} %copy-done), custom_call_target="tpu_custom_call" | custom-call | flops 3145728000 | bytes 9441280 | tf_op jit(solution)/shard_map/pallas_call | solution.py:183
  104.0 4.5 %all-to-all-start.2 = ((bf16[16,32,1024]{2,1,0:T(8,128)(2,1)}), bf16[16,32,1024]{2,1,0:T(8,128)(2,1)}, u32[]{:S(2)}, u32[]{:S(2)}) async-start(bf16[16,32,1024]{2,1,0:T(8,128)(2,1)} %bitcast.16), calls=%async_computation.2 | async-start | bytes 2097152 | tf_op jit(solution)/shard_map/all_to_all | solution.py:253
  113.3 3.9 %shard_map.63 = (bf16[64,1024]{1,0:T(8,128)(2,1)S(1)}, bf16[64,1024]{1,0:T(8,128)(2,1)S(1)}, bf16[64,1024]{1,0:T(8,128)(2,1)S(1)}, bf16[64,1024]{1,0:T(8,128)(2,...) custom-call(bf16[512,1024]{1,0:T(8,128)(2,1)S(1)} %copy-done.8, ...), custom_call_target="tpu_custom_call" | custom-call | flops 2097152000 | bytes 9179136 | tf_op jit(solution)/shard_map/pallas_call | solution.py:183
  125.8 3.6 %collective-permute-start.22 = (bf16[64,1024]{1,0:T(8,128)(2,1)S(1)}, bf16[64,1024]{1,0:T(8,128)(2,1)S(1)}, u32[]{:S(2)}, u32[]{:S(2)}) collective-permute-start(bf16[64,1024]{1,0:T(8,128)(2,1)S(1)} %get-tuple-element.39), channel_id=1, source_target_pairs={{0,28},{1,29},{2,30},{3,31},{4,24},{5,25},{6,26},{7,27},{8,20},{9,... | collective-permute-start | bytes 393224 | tf_op jit(solution)/shard_map/ppermute | solution.py:250
  129.3 9.5 %collective-permute-done.18.refs_2_ = bf16[64,1024]{1,0:T(8,128)(2,1)S(1)} collective-permute-done((bf16[64,1024]{1,0:T(8,128)(2,1)S(1)}, bf16[64,1024]{1,0:T(8,128)(2,1)S(1)}, u32[]{:S(2)}, u32[]{:S(2)}) %collective-permute-start.18) | collective-permute-done | bytes 131104 | tf_op jit(solution)/shard_map/ppermute | solution.py:250
  138.8 4.5 %collective-permute-start.23 = (bf16[64,1024]{1,0:T(8,128)(2,1)S(1)}, bf16[64,1024]{1,0:T(8,128)(2,1)S(1)}, u32[]{:S(2)}, u32[]{:S(2)}) collective-permute-start(bf16[64,1024]{1,0:T(8,128)(2,1)S(1)} %get-tuple-element.40), channel_id=1, source_target_pairs={{0,30},{1,31},{2,28},{3,29},{4,26},{5,27},{6,24},{7,25},{8,22},{9,... | collective-permute-start | bytes 393224 | tf_op jit(solution)/shard_map/ppermute | solution.py:250
  143.4 10.8 %collective-permute-start.17 = (bf16[64,1024]{1,0:T(8,128)(2,1)S(1)}, bf16[64,1024]{1,0:T(8,128)(2,1)S(1)}, u32[]{:S(2)}, u32[]{:S(2)}) collective-permute-start(bf16[64,1024]{1,0:T(8,128)(2,1)S(1)} %copy-done.31), channel_id=1, source_target_pairs={{0,18},{1,19},{2,16},{3,17},{4,22},{5,23},{6,20},{7,21},{8,26},{9,... | collective-permute-start | bytes 393224 | tf_op jit(solution)/shard_map/ppermute | solution.py:250
  154.8 10.1 %collective-permute-done.16.refs_0_ = bf16[64,1024]{1,0:T(8,128)(2,1)S(1)} collective-permute-done((bf16[64,1024]{1,0:T(8,128)(2,1)S(1)}, bf16[64,1024]{1,0:T(8,128)(2,1)S(1)}, u32[]{:S(2)}, u32[]{:S(2)}) %collective-permute-start.16) | collective-permute-done | bytes 131104 | tf_op jit(solution)/shard_map/ppermute | solution.py:250
  164.9 2.9 %collective-permute-done.17.refs_1_ = bf16[64,1024]{1,0:T(8,128)(2,1)S(1)} collective-permute-done((bf16[64,1024]{1,0:T(8,128)(2,1)S(1)}, bf16[64,1024]{1,0:T(8,128)(2,1)S(1)}, u32[]{:S(2)}, u32[]{:S(2)}) %collective-permute-start.17) | collective-permute-done | bytes 131104 | tf_op jit(solution)/shard_map/ppermute | solution.py:250
  169.8 3.5 %shard_map.65 = bf16[512,1024]{1,0:T(8,128)(2,1)} custom-call(bf16[64,1024]{1,0:T(8,128)(2,1)S(1)} %collective-permute-done.16.refs_0_, bf16[64,1024]{1,0:T(8,128)(2,1)S(1)} %collective-permute-done.17.refs_1_, bf16[64,1024]{1,0:T(8,128)(2,1)S(1)} %collective-permute-done.18.refs_2_, bf16[64,1024]{1,0:T(8,128)(2,1)S(1)} %collective-permute-done.19.refs_3_, ...), custom_call_target="tpu_custom_call" | custom-call | flops 1073741824 | bytes 4196352 | tf_op jit(solution)/shard_map/pallas_call | solution.py:183
  (144 shorter events, 47.4 us)
Async XLA Ops:
  2.3 14.5 %all-to-all-start.1 = ((s32[32,1,32]{2,1,0:T(1,128)}), s32[32,1,32]{2,1,0:T(1,128)S(1)}, u32[]{:S(2)}, u32[]{:S(2)}) async-start(s32[32,1,32]{2,1,0:T(1,128)} %bitcast.5), calls=%async_computation.1 | async-start | bytes 32768 | tf_op jit(solution)/shard_map/all_to_all | solution.py:272
  16.8 62.1 %all-to-all-start = ((bf16[16,32,1024]{2,1,0:T(8,128)(2,1)}), bf16[16,32,1024]{2,1,0:T(8,128)(2,1)S(1)}, u32[]{:S(2)}, u32[]{:S(2)}) async-start(bf16[16,32,1024]{2,1,0:T(8,128)(2,1)} %bitcast.2), calls=%async_computation | async-start | bytes 2097152 | tf_op jit(solution)/shard_map/all_to_all | solution.py:253
  20.4 16.5 %collective-permute-start.2 = (bf16[64,1024]{1,0:T(8,128)(2,1)S(1)}, bf16[64,1024]{1,0:T(8,128)(2,1)S(1)}, u32[]{:S(2)}, u32[]{:S(2)}) collective-permute-start(bf16[64,1024]{1,0:T(8,128)(2,1)S(1)} %copy-done.40), channel_id=1, source_target_pairs={{0,20},{1,21},{2,22},{3,23},{4,16},{5,17},{6,18},{7,19},{8,28},{9,... | collective-permute-start | bytes 393224 | tf_op jit(solution)/shard_map/ppermute | solution.py:250
  23.6 22.2 %collective-permute-start.3 = (bf16[64,1024]{1,0:T(8,128)(2,1)S(1)}, bf16[64,1024]{1,0:T(8,128)(2,1)S(1)}, u32[]{:S(2)}, u32[]{:S(2)}) collective-permute-start(bf16[64,1024]{1,0:T(8,128)(2,1)S(1)} %copy-done.39), channel_id=1, source_target_pairs={{0,22},{1,23},{2,20},{3,21},{4,18},{5,19},{6,16},{7,17},{8,30},{9,... | collective-permute-start | bytes 393224 | tf_op jit(solution)/shard_map/ppermute | solution.py:250
  25.6 22.8 %collective-permute-start.4 = (bf16[64,1024]{1,0:T(8,128)(2,1)S(1)}, bf16[64,1024]{1,0:T(8,128)(2,1)S(1)}, u32[]{:S(2)}, u32[]{:S(2)}) collective-permute-start(bf16[64,1024]{1,0:T(8,128)(2,1)S(1)} %copy-done.38), channel_id=1, source_target_pairs={{0,24},{1,25},{2,26},{3,27},{4,28},{5,29},{6,30},{7,31},{8,16},{9,... | collective-permute-start | bytes 393224 | tf_op jit(solution)/shard_map/ppermute | solution.py:250
  28.3 20.5 %collective-permute-start.5 = (bf16[64,1024]{1,0:T(8,128)(2,1)S(1)}, bf16[64,1024]{1,0:T(8,128)(2,1)S(1)}, u32[]{:S(2)}, u32[]{:S(2)}) collective-permute-start(bf16[64,1024]{1,0:T(8,128)(2,1)S(1)} %copy-done.37), channel_id=1, source_target_pairs={{0,26},{1,27},{2,24},{3,25},{4,30},{5,31},{6,28},{7,29},{8,18},{9,... | collective-permute-start | bytes 393224 | tf_op jit(solution)/shard_map/ppermute | solution.py:250
  29.1 22.6 %collective-permute-start.6 = (bf16[64,1024]{1,0:T(8,128)(2,1)S(1)}, bf16[64,1024]{1,0:T(8,128)(2,1)S(1)}, u32[]{:S(2)}, u32[]{:S(2)}) collective-permute-start(bf16[64,1024]{1,0:T(8,128)(2,1)S(1)} %copy-done.36), channel_id=1, source_target_pairs={{0,28},{1,29},{2,30},{3,31},{4,24},{5,25},{6,26},{7,27},{8,20},{9,... | collective-permute-start | bytes 393224 | tf_op jit(solution)/shard_map/ppermute | solution.py:250
  37.0 18.3 %collective-permute-start.7 = (bf16[64,1024]{1,0:T(8,128)(2,1)}, bf16[64,1024]{1,0:T(8,128)(2,1)S(1)}, u32[]{:S(2)}, u32[]{:S(2)}) collective-permute-start(bf16[64,1024]{1,0:T(8,128)(2,1)} %get-tuple-element.29), channel_id=1, source_target_pairs={{0,30},{1,31},{2,28},{3,29},{4,26},{5,27},{6,24},{7,25},{8,22},{9,... | collective-permute-start | bytes 393224 | tf_op jit(solution)/shard_map/ppermute | solution.py:250
  45.8 22.7 %collective-permute-start = (bf16[64,1024]{1,0:T(8,128)(2,1)S(1)}, bf16[64,1024]{1,0:T(8,128)(2,1)S(1)}, u32[]{:S(2)}, u32[]{:S(2)}) collective-permute-start(bf16[64,1024]{1,0:T(8,128)(2,1)S(1)} %copy-done.35), channel_id=1, source_target_pairs={{0,16},{1,17},{2,18},{3,19},{4,20},{5,21},{6,22},{7,23},{8,24},{9,... | collective-permute-start | bytes 393224 | tf_op jit(solution)/shard_map/ppermute | solution.py:250
  48.4 23.6 %collective-permute-start.1 = (bf16[64,1024]{1,0:T(8,128)(2,1)S(1)}, bf16[64,1024]{1,0:T(8,128)(2,1)S(1)}, u32[]{:S(2)}, u32[]{:S(2)}) collective-permute-start(bf16[64,1024]{1,0:T(8,128)(2,1)S(1)} %copy-done.34), channel_id=1, source_target_pairs={{0,18},{1,19},{2,16},{3,17},{4,22},{5,23},{6,20},{7,21},{8,26},{9,... | collective-permute-start | bytes 393224 | tf_op jit(solution)/shard_map/ppermute | solution.py:250
  48.8 23.2 %collective-permute-start.10 = (bf16[64,1024]{1,0:T(8,128)(2,1)S(1)}, bf16[64,1024]{1,0:T(8,128)(2,1)S(1)}, u32[]{:S(2)}, u32[]{:S(2)}) collective-permute-start(bf16[64,1024]{1,0:T(8,128)(2,1)S(1)} %collective-permute-done.2.refs_2_), channel_id=1, source_target_pairs={{0,1},{1,0},{2,3},{3,2},{4,5},{5,4},{6,7},{7,6},{8,9},{9,8},{10,11... | collective-permute-start | bytes 393224 | tf_op jit(solution)/shard_map/ppermute | solution.py:250
  51.6 20.9 %collective-permute-start.11 = (bf16[64,1024]{1,0:T(8,128)(2,1)S(1)}, bf16[64,1024]{1,0:T(8,128)(2,1)S(1)}, u32[]{:S(2)}, u32[]{:S(2)}) collective-permute-start(bf16[64,1024]{1,0:T(8,128)(2,1)S(1)} %collective-permute-done.3.refs_3_), channel_id=1, source_target_pairs={{0,1},{1,0},{2,3},{3,2},{4,5},{5,4},{6,7},{7,6},{8,9},{9,8},{10,11... | collective-permute-start | bytes 393224 | tf_op jit(solution)/shard_map/ppermute | solution.py:250
  55.3 17.3 %collective-permute-start.12 = (bf16[64,1024]{1,0:T(8,128)(2,1)S(1)}, bf16[64,1024]{1,0:T(8,128)(2,1)S(1)}, u32[]{:S(2)}, u32[]{:S(2)}) collective-permute-start(bf16[64,1024]{1,0:T(8,128)(2,1)S(1)} %collective-permute-done.4.refs_4_), channel_id=1, source_target_pairs={{0,1},{1,0},{2,3},{3,2},{4,5},{5,4},{6,7},{7,6},{8,9},{9,8},{10,11... | collective-permute-start | bytes 393224 | tf_op jit(solution)/shard_map/ppermute | solution.py:250
  104.0 65.8 %all-to-all-start.2 = ((bf16[16,32,1024]{2,1,0:T(8,128)(2,1)}), bf16[16,32,1024]{2,1,0:T(8,128)(2,1)}, u32[]{:S(2)}, u32[]{:S(2)}) async-start(bf16[16,32,1024]{2,1,0:T(8,128)(2,1)} %bitcast.16), calls=%async_computation.2 | async-start | bytes 2097152 | tf_op jit(solution)/shard_map/all_to_all | solution.py:253
  117.2 21.7 %collective-permute-start.18 = (bf16[64,1024]{1,0:T(8,128)(2,1)S(1)}, bf16[64,1024]{1,0:T(8,128)(2,1)S(1)}, u32[]{:S(2)}, u32[]{:S(2)}) collective-permute-start(bf16[64,1024]{1,0:T(8,128)(2,1)S(1)} %get-tuple-element.35), channel_id=1, source_target_pairs={{0,20},{1,21},{2,22},{3,23},{4,16},{5,17},{6,18},{7,19},{8,28},{9,... | collective-permute-start | bytes 393224 | tf_op jit(solution)/shard_map/ppermute | solution.py:250
  119.7 23.7 %collective-permute-start.19 = (bf16[64,1024]{1,0:T(8,128)(2,1)S(1)}, bf16[64,1024]{1,0:T(8,128)(2,1)S(1)}, u32[]{:S(2)}, u32[]{:S(2)}) collective-permute-start(bf16[64,1024]{1,0:T(8,128)(2,1)S(1)} %get-tuple-element.36), channel_id=1, source_target_pairs={{0,22},{1,23},{2,20},{3,21},{4,18},{5,19},{6,16},{7,17},{8,30},{9,... | collective-permute-start | bytes 393224 | tf_op jit(solution)/shard_map/ppermute | solution.py:250
  122.1 21.3 %collective-permute-start.20 = (bf16[64,1024]{1,0:T(8,128)(2,1)S(1)}, bf16[64,1024]{1,0:T(8,128)(2,1)S(1)}, u32[]{:S(2)}, u32[]{:S(2)}) collective-permute-start(bf16[64,1024]{1,0:T(8,128)(2,1)S(1)} %get-tuple-element.37), channel_id=1, source_target_pairs={{0,24},{1,25},{2,26},{3,27},{4,28},{5,29},{6,30},{7,31},{8,16},{9,... | collective-permute-start | bytes 393224 | tf_op jit(solution)/shard_map/ppermute | solution.py:250
  124.4 29.8 %collective-permute-start.21 = (bf16[64,1024]{1,0:T(8,128)(2,1)S(1)}, bf16[64,1024]{1,0:T(8,128)(2,1)S(1)}, u32[]{:S(2)}, u32[]{:S(2)}) collective-permute-start(bf16[64,1024]{1,0:T(8,128)(2,1)S(1)} %get-tuple-element.38), channel_id=1, source_target_pairs={{0,26},{1,27},{2,24},{3,25},{4,30},{5,31},{6,28},{7,29},{8,18},{9,... | collective-permute-start | bytes 393224 | tf_op jit(solution)/shard_map/ppermute | solution.py:250
  125.8 28.4 %collective-permute-start.22 = (bf16[64,1024]{1,0:T(8,128)(2,1)S(1)}, bf16[64,1024]{1,0:T(8,128)(2,1)S(1)}, u32[]{:S(2)}, u32[]{:S(2)}) collective-permute-start(bf16[64,1024]{1,0:T(8,128)(2,1)S(1)} %get-tuple-element.39), channel_id=1, source_target_pairs={{0,28},{1,29},{2,30},{3,31},{4,24},{5,25},{6,26},{7,27},{8,20},{9,... | collective-permute-start | bytes 393224 | tf_op jit(solution)/shard_map/ppermute | solution.py:250
  138.8 15.9 %collective-permute-start.23 = (bf16[64,1024]{1,0:T(8,128)(2,1)S(1)}, bf16[64,1024]{1,0:T(8,128)(2,1)S(1)}, u32[]{:S(2)}, u32[]{:S(2)}) collective-permute-start(bf16[64,1024]{1,0:T(8,128)(2,1)S(1)} %get-tuple-element.40), channel_id=1, source_target_pairs={{0,30},{1,31},{2,28},{3,29},{4,26},{5,27},{6,24},{7,25},{8,22},{9,... | collective-permute-start | bytes 393224 | tf_op jit(solution)/shard_map/ppermute | solution.py:250
  143.3 21.5 %collective-permute-start.16 = (bf16[64,1024]{1,0:T(8,128)(2,1)S(1)}, bf16[64,1024]{1,0:T(8,128)(2,1)S(1)}, u32[]{:S(2)}, u32[]{:S(2)}) collective-permute-start(bf16[64,1024]{1,0:T(8,128)(2,1)S(1)} %copy-done.33), channel_id=1, source_target_pairs={{0,16},{1,17},{2,18},{3,19},{4,20},{5,21},{6,22},{7,23},{8,24},{9,... | collective-permute-start | bytes 393224 | tf_op jit(solution)/shard_map/ppermute | solution.py:250
  143.4 24.4 %collective-permute-start.17 = (bf16[64,1024]{1,0:T(8,128)(2,1)S(1)}, bf16[64,1024]{1,0:T(8,128)(2,1)S(1)}, u32[]{:S(2)}, u32[]{:S(2)}) collective-permute-start(bf16[64,1024]{1,0:T(8,128)(2,1)S(1)} %copy-done.31), channel_id=1, source_target_pairs={{0,18},{1,19},{2,16},{3,17},{4,22},{5,23},{6,20},{7,21},{8,26},{9,... | collective-permute-start | bytes 393224 | tf_op jit(solution)/shard_map/ppermute | solution.py:250
  154.2 14.1 %collective-permute-start.27 = (bf16[64,1024]{1,0:T(8,128)(2,1)S(1)}, bf16[64,1024]{1,0:T(8,128)(2,1)S(1)}, u32[]{:S(2)}, u32[]{:S(2)}) collective-permute-start(bf16[64,1024]{1,0:T(8,128)(2,1)S(1)} %collective-permute-done.19.refs_3_), channel_id=1, source_target_pairs={{0,1},{1,0},{2,3},{3,2},{4,5},{5,4},{6,7},{7,6},{8,9},{9,8},{10,11... | collective-permute-start | bytes 393224 | tf_op jit(solution)/shard_map/ppermute | solution.py:250
  154.7 13.6 %collective-permute-start.28 = (bf16[64,1024]{1,0:T(8,128)(2,1)S(1)}, bf16[64,1024]{1,0:T(8,128)(2,1)S(1)}, u32[]{:S(2)}, u32[]{:S(2)}) collective-permute-start(bf16[64,1024]{1,0:T(8,128)(2,1)S(1)} %collective-permute-done.20.refs_4_), channel_id=1, source_target_pairs={{0,1},{1,0},{2,3},{3,2},{4,5},{5,4},{6,7},{7,6},{8,9},{9,8},{10,11... | collective-permute-start | bytes 393224 | tf_op jit(solution)/shard_map/ppermute | solution.py:250
  (52 other events, 351.9 us)
